TPU v7x, 512 devices: a whole 4x4x16 slice. The times are simulated.
512 devices in a mesh: tiles: 128 (over z, y, core), rep: 4 (over x).
Axes of the slice: x: 4, y: 4, z: 16, core: 2. Of those that a mesh axis runs over, the one named last changes fastest.
Arguments:
- tiles: bfloat16 [1024, 64, 4096], P(('tiles', 'rep')), may hold values from -6 to 6
- block_one: int32 [1024], P(('tiles', 'rep')), may hold values from 0 to 127
- block_two: int32 [1024], P(('tiles', 'rep')), may hold values from 0 to 255
- block_three: int32 [1024], P(('tiles', 'rep')), may hold values from 0 to 15
- owner_map: int32 [128], replicated, may hold values from 0 to 127, each once
- u_one: float32 [32, 8192], P(None, 'tiles'), may hold values from -6 to 6
- u_two: bfloat16 [32, 16384], P(None, 'tiles'), may hold values from -6 to 6
- u_three: bfloat16 [32, 1024], replicated, may hold values from -6 to 6
Outputs:
- factor: float32 [32, 8192], P(None, 'tiles')
- tile_factor: bfloat16 [1024, 2048], P(('tiles', 'rep'))
All inputs are finite; a program needn't handle non-finite values.
Results may differ from a plain program's by a relative error of at most 0.0081.
Values may be sent and summed in bfloat16 or wider, within the bound.
A program may use at most 64 MiB of HBM per device.

v0:
```python
import jax
import jax.numpy as jnp
from jax import lax
from jax.sharding import PartitionSpec as P

NS_STEPS = 2


def pick(table, index, width):
    grid = table.reshape(table.shape[0], -1, width)
    return jnp.transpose(jnp.take(grid, index, axis=1), (1, 0, 2))


def gram_total(local):
    return lax.psum(local, "tiles")


def orthonormal(rows, rows_total):
    hi = lax.Precision.HIGHEST
    rank = rows.shape[0]
    g0 = gram_total(jnp.dot(rows, rows.T, precision=hi, preferred_element_type=jnp.float32))
    msq = jnp.trace(g0) / rows_total
    inv = 1.0 / jnp.sqrt(msq + 1e-06)
    x = rows * inv
    g = g0 * (inv * inv) / rows_total
    eye = jnp.eye(rank, dtype=jnp.float32)
    for step in range(NS_STEPS):
        if step > 0:
            g = (
                gram_total(jnp.dot(x, x.T, precision=hi, preferred_element_type=jnp.float32))
                / rows_total
            )
        x = jnp.dot(1.5 * eye - 0.5 * g, x, precision=hi, preferred_element_type=jnp.float32)
    return x


def spread(current):
    cast = current.astype(jnp.bfloat16)
    return lax.all_gather(cast, "tiles", axis=1, tiled=True)


def per_device(tiles, block_one, block_two, block_three, owner_map, u_one, u_two, u_three):
    hi = lax.Precision.HIGHEST
    count = tiles.shape[0]
    width = tiles.shape[1]
    rank = u_three.shape[0]
    blocks_total = owner_map.shape[0]
    rows_total = blocks_total * width
    two_full = lax.all_gather(u_two, "tiles", axis=1, tiled=True)
    two_pick = pick(two_full, block_two, width)
    three_pick = pick(u_three, block_three, width)
    cube = tiles.reshape(count, width, width, width)
    first = jnp.einsum(
        "tijk,tsk->tijs", cube, three_pick, preferred_element_type=jnp.float32
    ).astype(jnp.bfloat16)
    second = jnp.einsum("tijs,trj->tirs", first, two_pick, preferred_element_type=jnp.float32)
    products = second.reshape(count, width, rank * rank).astype(jnp.bfloat16)
    positions = jnp.take(owner_map, block_one)
    onehot = (positions[:, None] == jnp.arange(blocks_total, dtype=jnp.int32)[None, :]).astype(
        jnp.float32
    )
    current = u_one
    readers = pick(spread(current), positions, width)
    partial_value = jnp.einsum("tic,tri->rc", products, readers, preferred_element_type=jnp.float32)
    project = lax.psum(partial_value, ("tiles", "rep")).astype(jnp.bfloat16)
    z_tile = jnp.einsum("rc,tic->tri", project, products, preferred_element_type=jnp.float32)
    term = jnp.einsum("tri,tn->rni", z_tile, onehot, precision=hi).reshape(rank, rows_total)
    rows = lax.psum_scatter(term, "tiles", scatter_dimension=1, tiled=True)
    rows = lax.psum(rows, "rep")
    current = orthonormal(rows, rows_total)
    tile_factor = pick(spread(current), positions, width).reshape(count, rank * width)
    return (current, tile_factor)


def solution(mesh):
    in_specs = (
        P(("tiles", "rep"), None, None),
        P(("tiles", "rep")),
        P(("tiles", "rep")),
        P(("tiles", "rep")),
        P(),
        P(None, "tiles"),
        P(None, "tiles"),
        P(),
    )
    out_specs = (P(None, "tiles"), P(("tiles", "rep"), None))
    return jax.shard_map(
        per_device, mesh=mesh, in_specs=in_specs, out_specs=out_specs, check_vma=False
    )
```

profile of v0, /device:TPU:1, one launch (start us, length us, event | category | flops | bytes accessed | tf_op | source)
XLA Modules:
  0.0 1633.5 jit_solution(5011610970250502089)
XLA Ops:
  7.2 0.0 copy-start
  7.2 0.0 all-gather.4.cloned.1.call-start
  7.2 0.7 all-gather.4.cloned.1.call-update
  7.9 0.0 reduce-scatter.4.cloned.1.call-start
  8.0 0.7 compare_select_fusion.3
  8.6 0.7 convert_bitcast_fusion.1
  9.3 1.0 reshape.51
  10.4 109.1 %all-gather = bf16[128,64,32]{1,2,0:T(8,128)(2,1)S(1)} all-gather(bf16[1,64,32]{1,2,0:T(8,128)(2,1)S(1)} %convert_bitcast_fusion.1), channel_id=1, replica_groups=mesh['tiles'=128,'rep'=4] {'tiles'}, dimensions={0}, use_global_device_ids=true | all-gather | bytes 528384 | tf_op jit(solution)/shard_map/all_gather | solution.py:39
  119.5 0.4 copy.31
  119.9 0.8 reshape.103
  120.7 1.1 reshape.53
  121.9 0.7 copy.32
  122.6 0.0 copy-start.4
  122.6 0.0 copy-start.2
  122.6 0.0 copy-start.3
  122.6 3.4 reshape.52
  126.1 0.0 copy-done
  126.1 0.6 gather_fusion
  126.7 0.0 copy-done.4
  126.7 0.6 gather_fusion.2
  127.3 0.0 copy-done.2
  127.3 0.6 gather_fusion.3
  127.9 0.0 copy-done.3
  128.0 2.0 fusion
  130.0 17.5 %all-gather.4.cloned.1.call-done = bf16[32,16384]{1,0:T(8,128)(2,1)} async-done(((bf16[32,128]{1,0:T(8,128)(2,1)}), bf16[32,16384]{1,0:T(8,128)(2,1)}) %all-gather.4.cloned.1.call-update) | async-done | bytes 1048592 | tf_op jit(solution)/shard_map/all_gather | solution.py:49
  147.5 3.0 reshape.50
  150.6 2.7 copy.27
  153.3 2.1 gather_fusion.1
  155.4 1.1 fusion.1
  156.5 0.2 copy.30
  156.7 0.2 convolution_bitcast_fusion.1
  157.0 102.8 %all-reduce.1 = bf16[32,1024]{1,0:T(8,128)(2,1)S(1)} all-reduce(f32[32,1024]{1,0:T(8,128)S(1)} %convolution_bitcast_fusion.1), channel_id=1, replica_groups=mesh['tiles'=128,'rep'=4] {'tiles','rep'}, use_global_device_ids=true, to_apply=%region_0.0 | all-reduce | flops 32768 | bytes 196608 | tf_op jit(solution)/shard_map/psum | solution.py:65
  259.7 0.2 convolution_bitcast_fusion.2
  259.9 1.0 convolution_bitcast_fusion
  261.0 4.4 copy.45
  265.4 0.0 reduce-scatter.4.cloned.1.call-update
  265.5 245.9 %reduce-scatter.4.cloned.1.call-done = f32[64,32]{1,0:T(8,128)} async-done(((f32[8192,32]{1,0:T(8,128)}), f32[64,32]{1,0:T(8,128)}) %reduce-scatter.4.cloned.1.call-update) | async-done | bytes 8208
  511.3 0.8 copy.44
  512.2 13.3 psum.29
  525.5 0.1 fusion.44
  525.6 500.6 %psum.30 = f32[32,32]{1,0:T(8,128)S(1)} all-reduce(f32[32,32]{1,0:T(8,128)S(1)} %fusion.44), channel_id=1, replica_groups=mesh['tiles'=128,'rep'=4] {'tiles'}, use_global_device_ids=true, to_apply=%region_3.5 | all-reduce | flops 1024 | bytes 8192 | tf_op jit(solution)/shard_map/psum | solution.py:15
  1026.3 0.6 select_reduce_fusion
  1027.6 0.1 fusion.6
  1027.7 0.2 fusion.45
  1027.9 490.9 %psum.31 = f32[32,32]{1,0:T(8,128)S(1)} all-reduce(f32[32,32]{1,0:T(8,128)S(1)} %fusion.45), channel_id=1, replica_groups=mesh['tiles'=128,'rep'=4] {'tiles'}, use_global_device_ids=true, to_apply=%region_5.7 | all-reduce | flops 1024 | bytes 8192 | tf_op jit(solution)/shard_map/psum | solution.py:15
  1518.7 0.1 fusion.7
  1518.9 0.0 copy-start.1
  1518.9 103.3 %all-gather.1 = bf16[128,64,32]{1,2,0:T(8,128)(2,1)S(1)} all-gather(bf16[1,64,32]{1,2,0:T(8,128)(2,1)S(1)} %convert_bitcast_fusion), channel_id=1, replica_groups=mesh['tiles'=128,'rep'=4] {'tiles'}, dimensions={0}, use_global_device_ids=true | all-gather | bytes 528384 | tf_op jit(solution)/shard_map/all_gather | solution.py:39
  1622.2 0.4 copy.37
  1622.6 0.8 reshape.105
  1623.5 0.0 copy-done.1
  1623.5 1.1 reshape.55
  1624.6 0.7 copy.38
  1625.3 0.6 gather_fusion.4
  1625.9 0.1 broadcast_select_fusion
  1625.9 0.7 reshape.56
  (12 shorter events, 0.1 us)
Async XLA Ops:
  7.2 118.9 %copy-start = (s32[128]{0:T(128)S(1)}, s32[128]{0:T(128)}, u32[]{:S(2)}) copy-start(s32[128]{0:T(128)} %param.14) | copy-start | bytes 1540
  7.2 140.3 %all-gather.4.cloned.1.call-start = ((), (), s32[]{:S(2)}) async-start(), calls=%async_computation.1 | async-start | bytes 1056768 | tf_op jit(solution)/shard_map/all_gather | solution.py:49
  7.9 503.4 %reduce-scatter.4.cloned.1.call-start = ((), (), s32[]{:S(2)}) async-start(), calls=%async_computation.2 | async-start | bytes 4227072
  122.6 4.2 copy-start.4
  122.6 4.7 copy-start.2
  122.6 5.3 copy-start.3
  1518.9 104.6 %copy-start.1 = (f32[32,64]{1,0:T(8,128)}, f32[32,64]{1,0:T(8,128)S(1)}, u32[]{:S(2)}) copy-start(f32[32,64]{1,0:T(8,128)S(1)} %fusion.7) | copy-start | bytes 24580
Sparse Core Ops, SparseCore 0:
  11.0 136.4 all-gather.3
  265.6 245.7 reduce-scatter.3
where the time goes:
time: 1630 us
  blocking collectives  1320 us (81%)
  waiting for transfers between devices  264 us (16%)
  local copies, waits for them, and re-layouts  27 us (2%)
    psum x2, blocking collectives, gram_total(): return lax.psum(local, 'tiles')  992 us
    unnamed x3, waiting for transfers between devices  247 us
    all_gather x2, blocking collectives, spread(): return lax.all_gather(cast, 'tiles', axis=1, tiled=True)  212 us
    psum x1, blocking collectives, per_device(): project = lax.psum(partial_value, ('tiles', 'rep')).astype(jnp.bfloat16)  103 us
  transfers between devices with their start and end apart: 2, of which 2 were waited for; matrix products, arithmetic and copies ran while one was open for 1% of the time, Pallas kernels for 0%

commit v1 on v0

--- a/solution.py
+++ b/solution.py
@@ -1,9 +1,18 @@
+import functools
 import jax
 import jax.numpy as jnp
 from jax import lax
 from jax.sharding import PartitionSpec as P
 
 NS_STEPS = 2
+
+
+def connect_blocks_by_axis(w_in, across):
+    step_out = jnp.stack(jax.lax.psum(1, across) * [w_in], 0)
+    return jnp.concatenate(jax.lax.all_to_all(step_out, across, 0, 0), 1)
+
+
+supply_series = functools.partial(connect_blocks_by_axis, across="tiles")
 
 
 def pick(table, index, width):
@@ -36,7 +45,7 @@
 
 def spread(current):
     cast = current.astype(jnp.bfloat16)
-    return lax.all_gather(cast, "tiles", axis=1, tiled=True)
+    return supply_series(cast)
 
 
 def per_device(tiles, block_one, block_two, block_three, owner_map, u_one, u_two, u_three):

time: 1630 us -> 1580 us (0.969)
  blocking collectives: 1320 us -> 1160 us
  waiting for transfers between devices: 264 us -> 359 us
  starting transfers between devices: 0.08 us -> 21.1 us
    all_gather x2 -> x0, blocking collectives: 212 us -> none  [spread(): return lax.all_gather(cast, 'tiles', axis=1, tiled=True)]
    all_gather x1, waiting for transfers between devices: 17.5 us -> 113 us  [per_device(): two_full = lax.all_gather(u_two, 'tiles', axis=1, tiled=True)]
    all_to_all x0 -> x1, blocking collectives: none -> 47.5 us  [connect_blocks_by_axis(): return jnp.concatenate(jax.lax.all_to_all(step_out, across, 0, 0), 1)]
    all_to_all x0 -> x1, starting transfers between devices: none -> 21 us  [connect_blocks_by_axis(): return jnp.concatenate(jax.lax.all_to_all(step_out, across, 0, 0), 1)]
  transfers between devices with their start and end apart: 2 -> 3, of which waited for: 2 -> 2; matrix products, arithmetic and copies ran while one was open for 1% -> 1% of each run, Pallas kernels for 0% -> 0%
where the time goes in v1:
time: 1580 us
  blocking collectives  1160 us (73%)
  waiting for transfers between devices  359 us (23%)
  local copies, waits for them, and re-layouts  24.1 us (2%)
  starting transfers between devices  21.1 us (1%)
    psum x2, blocking collectives, gram_total(): return lax.psum(local, 'tiles')  991 us
    unnamed x3, waiting for transfers between devices  246 us
    all_gather x1, waiting for transfers between devices, per_device(): two_full = lax.all_gather(u_two, 'tiles', axis=1, tiled=True)  113 us
    psum x1, blocking collectives, per_device(): project = lax.psum(partial_value, ('tiles', 'rep')).astype(jnp.bfloat16)  103 us
    all_to_all x1, blocking collectives, connect_blocks_by_axis(): return jnp.concatenate(jax.lax.all_to_all(step_out, across, 0, 0), 1)  47.5 us
  transfers between devices with their start and end apart: 3, of which 2 were waited for; matrix products, arithmetic and copies ran while one was open for 1% of the time, Pallas kernels for 0%

profile of v1, /device:TPU:1, one launch (start us, length us, event | category | flops | bytes accessed | tf_op | source)
XLA Modules:
  0.0 1581.6 jit_solution(9080636432979419780)
XLA Ops:
  7.2 0.0 copy-start
  7.2 0.0 copy-start.3
  7.2 0.0 copy-start.5
  7.2 0.0 copy-start.2
  7.2 0.0 copy-start.1
  7.2 0.0 all-gather.2.cloned.1.call-start
  7.3 0.7 all-gather.2.cloned.1.call-update
  8.0 0.7 convert_element_type.31
  8.7 0.1 stack.4
  8.8 1.4 reshape.117
  10.2 21.0 %all-to-all-start = ((bf16[128,2,1024]{2,1,0:T(2,128)(2,1)}), bf16[128,2,1024]{2,1,0:T(2,128)(2,1)}, u32[]{:S(2)}, u32[]{:S(2)}) async-start(bf16[128,2,1024]{2,1,0:T(2,128)(2,1)} %reshape.117), calls=%async_computation | async-start | bytes 1048576 | tf_op jit(solution)/shard_map/all_to_all | solution.py:12
  31.3 0.0 copy-start.4
  31.3 0.0 reduce-scatter.4.cloned.1.call-start
  31.3 0.0 copy-done.3
  31.4 0.0 copy-done.5
  31.4 0.0 copy-done.2
  31.4 0.1 reshape.55
  31.6 0.0 copy-done.1
  31.6 2.3 reshape.56
  33.9 0.0 copy-done
  33.9 0.6 gather_fusion
  34.6 0.6 gather_fusion.2
  35.1 0.0 copy-done.4
  35.2 2.0 fusion
  37.3 112.8 %all-gather.2.cloned.1.call-done = bf16[32,16384]{1,0:T(8,128)(2,1)} async-done(((bf16[32,128]{1,0:T(8,128)(2,1)}), bf16[32,16384]{1,0:T(8,128)(2,1)}) %all-gather.2.cloned.1.call-update) | async-done | bytes 1048592 | tf_op jit(solution)/shard_map/all_gather | solution.py:58
  150.1 3.0 reshape.54
  153.1 2.7 copy.21
  155.8 2.1 gather_fusion.1
  158.0 1.1 fusion.1
  159.0 0.2 copy.24
  159.3 0.0 all-to-all-done
  159.3 2.3 reshape.118
  161.5 0.6 gather_fusion.3
  162.1 0.2 convolution_bitcast_fusion.1
  162.3 102.8 %all-reduce.1 = bf16[32,1024]{1,0:T(8,128)(2,1)S(1)} all-reduce(f32[32,1024]{1,0:T(8,128)S(1)} %convolution_bitcast_fusion.1), channel_id=1, replica_groups=mesh['tiles'=128,'rep'=4] {'tiles','rep'}, use_global_device_ids=true, to_apply=%region_0.0 | all-reduce | flops 32768 | bytes 196608 | tf_op jit(solution)/shard_map/psum | solution.py:74
  265.2 0.2 convolution_bitcast_fusion.2
  265.4 1.0 convolution_bitcast_fusion
  266.4 4.4 copy.35
  270.9 0.0 reduce-scatter.4.cloned.1.call-update
  270.9 245.6 %reduce-scatter.4.cloned.1.call-done = f32[64,32]{1,0:T(8,128)} async-done(((f32[8192,32]{1,0:T(8,128)}), f32[64,32]{1,0:T(8,128)}) %reduce-scatter.4.cloned.1.call-update) | async-done | bytes 8208
  516.5 0.8 copy.34
  517.3 13.3 psum.29
  530.6 0.1 fusion.45
  530.7 500.6 %psum.30 = f32[32,32]{1,0:T(8,128)S(1)} all-reduce(f32[32,32]{1,0:T(8,128)S(1)} %fusion.45), channel_id=1, replica_groups=mesh['tiles'=128,'rep'=4] {'tiles'}, use_global_device_ids=true, to_apply=%region_3.5 | all-reduce | flops 1024 | bytes 8192 | tf_op jit(solution)/shard_map/psum | solution.py:24
  1031.3 0.6 select_reduce_fusion
  1032.6 0.1 fusion.6
  1032.8 0.2 fusion.46
  1032.9 490.9 %psum.31 = f32[32,32]{1,0:T(8,128)S(1)} all-reduce(f32[32,32]{1,0:T(8,128)S(1)} %fusion.46), channel_id=1, replica_groups=mesh['tiles'=128,'rep'=4] {'tiles'}, use_global_device_ids=true, to_apply=%region_5.7 | all-reduce | flops 1024 | bytes 8192 | tf_op jit(solution)/shard_map/psum | solution.py:24
  1523.8 0.7 fusion.44
  1524.6 0.1 stack.5
  1524.7 0.6 reshape.119
  1525.3 47.5 %all_to_all.10 = bf16[128,2,1024]{2,1,0:T(2,128)(2,1)S(1)} all-to-all(bf16[128,2,1024]{2,1,0:T(2,128)(2,1)S(1)} %reshape.119), channel_id=1, replica_groups=mesh['tiles'=128,'rep'=4] {'tiles'}, dimensions={0} | all-to-all | bytes 1048576 | tf_op jit(solution)/shard_map/all_to_all | solution.py:12
  1572.8 0.6 reshape.120
  1573.4 0.6 gather_fusion.4
  1574.0 0.1 broadcast_select_fusion
  1574.0 0.7 reshape.60
  (12 shorter events, 0.1 us)
Async XLA Ops:
  7.2 26.7 %copy-start = (s32[128]{0:T(128)S(1)}, s32[128]{0:T(128)}, u32[]{:S(2)}) copy-start(s32[128]{0:T(128)} %param.14) | copy-start | bytes 1540
  7.2 24.2 %copy-start.3 = (s32[2]{0:T(128)S(1)}, s32[2]{0:T(128)}, u32[]{:S(2)}) copy-start(s32[2]{0:T(128)} %param.11) | copy-start | bytes 28
  7.2 24.2 %copy-start.5 = (s32[2]{0:T(128)S(1)}, s32[2]{0:T(128)}, u32[]{:S(2)}) copy-start(s32[2]{0:T(128)} %param.13) | copy-start | bytes 28
  7.2 24.2 %copy-start.2 = (bf16[32,1024]{1,0:T(8,128)(2,1)S(1)}, bf16[32,1024]{1,0:T(8,128)(2,1)}, u32[]{:S(2)}) copy-start(bf16[32,1024]{1,0:T(8,128)(2,1)} %param.17) | copy-start | bytes 196612
  7.2 24.4 %copy-start.1 = (bf16[2,64,4096]{2,1,0:T(8,128)(2,1)S(1)}, bf16[2,64,4096]{2,1,0:T(8,128)(2,1)}, u32[]{:S(2)}) copy-start(bf16[2,64,4096]{2,1,0:T(8,128)(2,1)} %param.10) | copy-start | bytes 3145732
  7.2 142.8 %all-gather.2.cloned.1.call-start = ((), (), s32[]{:S(2)}) async-start(), calls=%async_computation.3 | async-start | bytes 1056768 | tf_op jit(solution)/shard_map/all_gather | solution.py:58
  10.2 149.0 %all-to-all-start = ((bf16[128,2,1024]{2,1,0:T(2,128)(2,1)}), bf16[128,2,1024]{2,1,0:T(2,128)(2,1)}, u32[]{:S(2)}, u32[]{:S(2)}) async-start(bf16[128,2,1024]{2,1,0:T(2,128)(2,1)} %reshape.117), calls=%async_computation | async-start | bytes 1048576 | tf_op jit(solution)/shard_map/all_to_all | solution.py:12
  31.3 3.8 copy-start.4
  31.3 485.2 %reduce-scatter.4.cloned.1.call-start = ((), (), s32[]{:S(2)}) async-start(), calls=%async_computation.4 | async-start | bytes 4227072
Sparse Core Ops, SparseCore 0:
  11.1 138.9 all-gather.1
  271.0 245.4 reduce-scatter.3
